TPU v7x, 32 devices: a whole 2x2x4 slice. The times are simulated.
32 devices in a mesh: dp: 4 (over y, core), bucket: 8 (over z, x).
Axes of the slice: x: 2, y: 2, z: 4, core: 2. Of those that a mesh axis runs over, the one named last changes fastest.
Arguments:
- frames: bfloat16 [49152, 512], P(('dp', 'bucket')), may hold values from -60 to 60, as said below
- lengths: int32 [4, 256], P('dp'), may hold values from 1 to 48, as said below
- owners: int32 [4, 256], P('dp'), may hold values from 0 to 7, as said below
- upstream: bfloat16 [24576, 512], P(('dp', 'bucket')), may hold values from -6 to 6
- ln_gain: float32 [512], replicated, may hold values from 0.1 to 1.9
- w_in: bfloat16 [512, 1024], replicated, may hold values from -0.25 to 0.25
- w_dw: float32 [512, 31], replicated, may hold values from -1 to 1
- bn_gain: float32 [512], replicated, may hold values from 0.1 to 1.9
- bn_bias: float32 [512], replicated, may hold values from -3 to 3
- w_out: bfloat16 [512, 512], replicated, may hold values from -0.25 to 0.25
Outputs:
- out_frames: bfloat16 [24576, 512], P(('dp', 'bucket'))
- grad_frames: bfloat16 [49152, 512], P(('dp', 'bucket'))
- grad_w_in: float32 [512, 1024], P('bucket')
- grad_w_out: float32 [512, 512], P('bucket')
- grad_w_dw: float32 [512, 31], P('bucket')
- grad_ln_gain: float32 [512], P('bucket')
- grad_bn_gain: float32 [512], replicated
- grad_bn_bias: float32 [512], replicated
Inputs may be any that keep to these rules, and one draw needn't show every extreme that they name: `frames`: frame rows past an utterance's length are not read. In each group every owner receives exactly 4 utterances from each loader shard, their lengths sum to exactly 768 with one of exactly 48, and the lengths an owner receives do not fall with the loader index. `owners`: in each group and loader shard every owner index appears exactly 4 times.
All inputs are finite; a program needn't handle non-finite values.
Results may differ from a plain program's by a relative error of at most 0.013.
Values may be sent and summed in bfloat16 or wider, within the bound.
A program may use at most 128 MiB of HBM per device.

v0:
```python
import jax
import jax.numpy as jnp
from jax import lax
from jax.sharding import PartitionSpec as P

EPSILON = 1e-05


def normalize_rows(frame_rows, ln_gain):
    values = frame_rows.astype(jnp.float32)
    centred = values - jnp.mean(values, axis=1, keepdims=True)
    inverse = lax.rsqrt(jnp.mean(centred * centred, axis=1, keepdims=True) + EPSILON)
    normed = centred * inverse
    return ((normed * ln_gain).astype(jnp.bfloat16), normed, inverse)


def normalize_back(grad_h, normed, inverse, ln_gain):
    scaled = grad_h * ln_gain
    inner_sum = jnp.mean(scaled * normed, axis=1, keepdims=True)
    return inverse * (scaled - jnp.mean(scaled, axis=1, keepdims=True) - normed * inner_sum)


def conv_forward(gated_rows, segment, w_dw):
    width_half = w_dw.shape[1] // 2
    length_all = gated_rows.shape[1]
    padded = jnp.pad(gated_rows, ((0, 0), (width_half, width_half), (0, 0)))
    seg_pad = jnp.pad(segment, ((0, 0), (width_half, width_half)), constant_values=-1)
    result = jnp.zeros(gated_rows.shape, jnp.float32)
    for offset in range(w_dw.shape[1]):
        same_seg = (seg_pad[:, offset : offset + length_all] == segment)[:, :, None]
        shifted = padded[:, offset : offset + length_all].astype(jnp.float32)
        result = result + jnp.where(same_seg, shifted, 0.0) * w_dw[:, offset]
    return result


def conv_backward(grad_conv, gated_rows, segment, w_dw):
    width_half = w_dw.shape[1] // 2
    length_all = gated_rows.shape[1]
    padded = jnp.pad(gated_rows, ((0, 0), (width_half, width_half), (0, 0)))
    grad_pad = jnp.pad(grad_conv, ((0, 0), (width_half, width_half), (0, 0)))
    seg_pad = jnp.pad(segment, ((0, 0), (width_half, width_half)), constant_values=-1)
    grad_gated = jnp.zeros(grad_conv.shape, jnp.float32)
    grad_cols = []
    for offset in range(w_dw.shape[1]):
        same_fwd = (seg_pad[:, offset : offset + length_all] == segment)[:, :, None]
        shifted = jnp.where(
            same_fwd, padded[:, offset : offset + length_all].astype(jnp.float32), 0.0
        )
        grad_cols.append(jnp.sum(shifted * grad_conv, axis=(0, 1)))
        back_start = 2 * width_half - offset
        same_back = (seg_pad[:, back_start : back_start + length_all] == segment)[:, :, None]
        grad_gated = (
            grad_gated
            + jnp.where(same_back, grad_pad[:, back_start : back_start + length_all], 0.0)
            * w_dw[:, offset]
        )
    return (grad_gated, jnp.stack(grad_cols, axis=1))


def local(frames, lengths, owners, upstream, ln_gain, w_in, w_dw, bn_gain, bn_bias, w_out):
    loaders = lax.axis_size("bucket")
    own_index = lax.axis_index("bucket")
    feature_count = frames.shape[1]
    slot_count = lengths.shape[1] // loaders
    span_max = frames.shape[0] // slot_count
    pair_count = slot_count // loaders
    own_rows = upstream.shape[0]
    total_frames = float(own_rows * loaders * lax.axis_size("dp"))
    lens_all = lengths[0].reshape(loaders, slot_count)
    dest_all = owners[0].reshape(loaders, slot_count)
    owner_ids = jnp.arange(loaders, dtype=jnp.int32)
    onehot = (dest_all[:, :, None] == owner_ids[None, None, :]).astype(jnp.int32)
    earlier = jnp.cumsum(onehot, axis=1) - onehot
    ranking = jnp.sum(earlier * onehot, axis=2)
    send_pos = dest_all * pair_count + ranking
    my_pos = lax.dynamic_index_in_dim(send_pos, own_index, 0, keepdims=False)
    send_order = (
        jnp.zeros((slot_count,), jnp.int32).at[my_pos].set(jnp.arange(slot_count, dtype=jnp.int32))
    )
    slot_frames = frames.reshape(slot_count, span_max, feature_count)
    outgoing = jnp.take(slot_frames, send_order, axis=0).reshape(
        loaders, pair_count, span_max, feature_count
    )
    incoming = lax.all_to_all(outgoing, "bucket", split_axis=0, concat_axis=0, tiled=True)
    incoming_rows = incoming.reshape(slot_count * span_max, feature_count)
    pair_ids = jnp.arange(pair_count, dtype=jnp.int32)
    to_me = (dest_all == own_index)[:, :, None] & (ranking[:, :, None] == pair_ids[None, None, :])
    recv_lens = jnp.sum(jnp.where(to_me, lens_all[:, :, None], 0), axis=1).reshape(-1)
    starts = jnp.cumsum(recv_lens) - recv_lens
    position = jnp.arange(span_max, dtype=jnp.int32)
    slot_valid = position[None, :] < recv_lens[:, None]
    row_ids = jnp.arange(own_rows, dtype=jnp.int32)
    row_slot = jnp.sum((starts[None, :] <= row_ids[:, None]).astype(jnp.int32), axis=1) - 1
    row_offset = row_ids - jnp.take(starts, row_slot)
    packed_source = row_slot * span_max + row_offset
    slot_target = jnp.minimum(
        jnp.where(slot_valid, starts[:, None] + position[None, :], own_rows - 1), own_rows - 1
    ).reshape(-1)
    slot_valid_flat = slot_valid.reshape(-1)
    segment = jnp.broadcast_to(
        jnp.arange(slot_count, dtype=jnp.int32)[:, None], (slot_count, span_max)
    )
    work_grad = jnp.where(slot_valid_flat[:, None], jnp.take(upstream, slot_target, axis=0), 0)
    group_count = segment.shape[0]
    group_length = segment.shape[1]
    normed_h, normed, inverse = normalize_rows(incoming_rows, ln_gain)
    projected = jnp.dot(normed_h, w_in, preferred_element_type=jnp.float32)
    linear = projected[:, :feature_count]
    gate_sig = jax.nn.sigmoid(projected[:, feature_count:])
    gated_rows = jnp.where(slot_valid_flat[:, None], linear * gate_sig, 0.0).astype(jnp.bfloat16)
    gated_blocks = gated_rows.reshape(group_count, group_length, feature_count)
    conv_rows = conv_forward(gated_blocks, segment, w_dw).reshape(-1, feature_count)
    masked = jnp.where(slot_valid_flat[:, None], conv_rows, 0.0)
    first_sum, second_sum = lax.psum(
        (jnp.sum(masked, axis=0), jnp.sum(masked * masked, axis=0)), ("dp", "bucket")
    )
    centre = first_sum / total_frames
    variance = second_sum / total_frames - centre * centre
    bn_inverse = lax.rsqrt(variance + EPSILON)
    bn_normed = (conv_rows - centre) * bn_inverse
    bn_value = bn_normed * bn_gain + bn_bias
    bn_sig = jax.nn.sigmoid(bn_value)
    swished = (bn_value * bn_sig).astype(jnp.bfloat16)
    out_rows = jnp.dot(swished, w_out, preferred_element_type=jnp.float32).astype(jnp.bfloat16)
    out_frames = jnp.take(out_rows, packed_source, axis=0)
    grad_wout = jnp.einsum("rd,re->de", swished, work_grad, preferred_element_type=jnp.float32)
    grad_swish = jnp.einsum("re,de->rd", work_grad, w_out, preferred_element_type=jnp.float32)
    grad_bn_rows = grad_swish * (bn_sig * (1.0 + bn_value * (1.0 - bn_sig)))
    bias_total, gain_total = lax.psum(
        (jnp.sum(grad_bn_rows, axis=0), jnp.sum(grad_bn_rows * bn_normed, axis=0)), ("dp", "bucket")
    )
    grad_conv = jnp.where(
        slot_valid_flat[:, None],
        bn_gain
        * bn_inverse
        * (grad_bn_rows - bias_total / total_frames - bn_normed * (gain_total / total_frames)),
        0.0,
    )
    grad_gated, grad_wdw = conv_backward(
        grad_conv.reshape(group_count, group_length, feature_count), gated_blocks, segment, w_dw
    )
    grad_gated = jnp.where(slot_valid_flat[:, None], grad_gated.reshape(-1, feature_count), 0.0)
    grad_proj = jnp.concatenate(
        [grad_gated * gate_sig, grad_gated * linear * gate_sig * (1.0 - gate_sig)], axis=1
    ).astype(jnp.bfloat16)
    grad_win = jnp.einsum("rd,rf->df", normed_h, grad_proj, preferred_element_type=jnp.float32)
    grad_h = jnp.einsum("rf,df->rd", grad_proj, w_in, preferred_element_type=jnp.float32)
    grad_ln = jnp.sum(grad_h * normed, axis=0)
    grad_work = jnp.where(
        slot_valid_flat[:, None], normalize_back(grad_h, normed, inverse, ln_gain), 0.0
    ).astype(jnp.bfloat16)
    returned = lax.all_to_all(
        grad_work.reshape(loaders, pair_count, span_max, feature_count),
        "bucket",
        split_axis=0,
        concat_axis=0,
        tiled=True,
    )
    grad_frames = jnp.take(
        returned.reshape(slot_count, span_max, feature_count), my_pos, axis=0
    ).reshape(-1, feature_count)
    row_sums = (
        lax.psum_scatter(grad_win, "bucket", scatter_dimension=0, tiled=True),
        lax.psum_scatter(grad_wout, "bucket", scatter_dimension=0, tiled=True),
        lax.psum_scatter(grad_wdw, "bucket", scatter_dimension=0, tiled=True),
        lax.psum_scatter(grad_ln, "bucket", scatter_dimension=0, tiled=True),
    )
    shares = (
        lax.psum(row_sums[0].astype(jnp.bfloat16), "dp").astype(jnp.float32),
        lax.psum(row_sums[1].astype(jnp.bfloat16), "dp").astype(jnp.float32),
        lax.psum(row_sums[2].astype(jnp.bfloat16), "dp").astype(jnp.float32),
        lax.psum(row_sums[3].astype(jnp.bfloat16), "dp").astype(jnp.float32),
    )
    return (
        out_frames,
        grad_frames,
        shares[0],
        shares[1],
        shares[2],
        shares[3],
        gain_total,
        bias_total,
    )


def solution(mesh):
    placed = (
        P(("dp", "bucket"), None),
        P("dp", None),
        P("dp", None),
        P(("dp", "bucket"), None),
        P(),
        P(),
        P(),
        P(),
        P(),
        P(),
    )
    return jax.shard_map(
        local,
        mesh=mesh,
        in_specs=placed,
        out_specs=(
            P(("dp", "bucket"), None),
            P(("dp", "bucket"), None),
            P("bucket", None),
            P("bucket", None),
            P("bucket", None),
            P("bucket"),
            P(),
            P(),
        ),
        check_vma=False,
    )
```

profile of v0, /device:TPU:0, one launch (start us, length us, event | category | flops | bytes accessed | tf_op | source)
XLA Modules:
  0.0 468.8 jit_solution(478238532868027686)
XLA Ops:
  15.4 7.3 %all-to-all-start = ((bf16[8,4,48,512]{3,2,1,0:T(8,128)(2,1)}), bf16[8,4,48,512]{3,2,1,0:T(8,128)(2,1)}, u32[]{:S(2)}, u32[]{:S(2)}) async-start(bf16[8,4,48,512]{3,2,1,0:T(8,128)(2,1)} %bitcast.243), calls=%async_computation | async-start | bytes 3145728 | tf_op jit(solution)/shard_map/all_to_all | solution.py:84
  24.5 5.4 %gather_fusion.1 = bf16[1536,512]{1,0:T(8,128)(2,1)} fusion(bf16[768,512]{1,0:T(8,128)(2,1)S(1)} %copy-done.1, s32[2048]{0:T(1024)S(1)} %pad_clamp_fusion), kind=kCustom, calls=%fused_computation.3 | custom fusion | bytes 3151872 | tf_op jit(solution)/shard_map/jit(_take)/gather | solution.py:103
  30.1 29.7 %all-to-all-done = bf16[8,4,48,512]{3,2,1,0:T(8,128)(2,1)} async-done(((bf16[8,4,48,512]{3,2,1,0:T(8,128)(2,1)}), bf16[8,4,48,512]{3,2,1,0:T(8,128)(2,1)}, u32[]{:S(2)}, u32[]{:S(2)}) %all-to-all-start) | async-done | bytes 1572896 | tf_op jit(solution)/shard_map/all_to_all | solution.py:84
  70.6 20.7 %select_reduce_fusion = (f32[512]{0:T(512)S(1)}, f32[512]{0:T(512)S(1)}, f32[32,48,512]{2,1,0:T(8,128)}) fusion(pred[32,48]{1,0:T(8,128)(4,1)S(1)} %iota_compare_fusion.3, f32[512]{0:T(512)S(1)} %bitcast.355, pred[32,48]{1,0:T(8,128)(4,1)S(1)} %bitcast.323, f32[512]{0:T(512)S(1)} %bitcast.357, pred[32,48]{1,0:T(8,128)(4,1)S(1)} %bitcast.320, ...), kind=kLoop, calls=%fused_computation.243 | loop fusion | flops 99089408 | bytes 4833792 | tf_op jit(solution)/shard_map/reduce_sum | solution.py:115
  91.3 37.9 %all-reduce.4 = (f32[512]{0:T(512)S(1)}, f32[512]{0:T(512)S(1)}) all-reduce(f32[512]{0:T(512)S(1)} %get-tuple-element.42, f32[512]{0:T(512)S(1)} %get-tuple-element.41), channel_id=1, replica_groups=mesh['dp'=4,'bucket'=8] {'dp','bucket'}, use_global_device_ids=true, to_apply=%region_11.13 | all-reduce | flops 1024 | bytes 8192 | tf_op jit(solution)/shard_map/psum | solution.py:114
  129.2 4.2 multiply_convert_fusion.2
  133.4 4.3 fusion.111
  137.7 41.4 %all-reduce.3 = (f32[512]{0:T(512)S(1)}, f32[512]{0:T(512)S(1)}) all-reduce(f32[512]{0:T(512)S(1)} %get-tuple-element.45, f32[512]{0:T(512)S(1)} %get-tuple-element.44), channel_id=1, replica_groups=mesh['dp'=4,'bucket'=8] {'dp','bucket'}, use_global_device_ids=true, to_apply=%region_15.17 | all-reduce | flops 1024 | bytes 8192 | tf_op jit(solution)/shard_map/psum | solution.py:129
  179.6 5.5 %multiply_reduce_fusion.16 = (f32[512]{0:T(512)S(1)}, f32[1536,512]{1,0:T(8,128)S(1)}) fusion(f32[1536,512]{1,0:T(8,128)} %copy-done.4, f32[512]{0:T(512)S(1)} %get-tuple-element.164, f32[1536,512]{1,0:T(8,128)} %get-tuple-element.162, f32[512]{0:T(512)S(1)} %get-tuple-element.165, f32[512]{0:T(512)S(1)} %get-tuple-element.83, pred[1536]{0:T(1024)(128)(4,1)S(1)} %lt.126, ...), kind=kLoop, calls=%fused_computation.182 | loop fusion | flops 11009536 | bytes 15738368 | tf_op jit(solution)/shard_map/reduce_sum | solution.py:49
  187.1 7.1 %multiply_reduce_fusion.10 = (f32[512]{0:T(512)S(1)}, f32[512]{0:T(512)S(1)}, f32[512]{0:T(512)S(1)}, f32[512]{0:T(512)S(1)}, f32[512]{0:T(512)S(1)}, /*index=5*...) fusion(f32[32,48,512]{2,1,0:T(8,128)S(1)} %bitcast.234, pred[32,48]{1,0:T(8,128)(4,1)S(1)} %bitcast.297, ...), kind=kLoop, calls=%fused_computation.176 | loop fusion | flops 28306944 | bytes 4750848 | tf_op jit(solution)/shard_map/reduce_sum | solution.py:49
  194.2 6.7 %multiply_reduce_fusion.20 = (f32[512]{0:T(512)S(1)}, f32[512]{0:T(512)S(1)}, f32[512]{0:T(512)S(1)}, f32[512]{0:T(512)S(1)}, f32[512]{0:T(512)S(1)}, /*index=5*...) fusion(f32[32,48,512]{2,1,0:T(8,128)S(1)} %bitcast.235, pred[32,48]{1,0:T(8,128)(4,1)S(1)} %bitcast.270, ...), kind=kLoop, calls=%fused_computation.186 | loop fusion | flops 28306944 | bytes 4750848 | tf_op jit(solution)/shard_map/reduce_sum | solution.py:49
  200.9 6.5 %multiply_reduce_fusion.1 = (f32[512]{0:T(512)S(1)}, f32[512]{0:T(512)S(1)}, f32[512]{0:T(512)S(1)}, f32[512]{0:T(512)S(1)}, f32[512]{0:T(512)S(1)}, /*index=5*/...) fusion(f32[32,48,512]{2,1,0:T(8,128)S(1)} %bitcast.236, pred[32,48]{1,0:T(8,128)(4,1)S(1)} %bitcast.324, ...), kind=kLoop, calls=%fused_computation.167 | loop fusion | flops 28306944 | bytes 4750848 | tf_op jit(solution)/shard_map/reduce_sum | solution.py:49
  208.5 4.0 fusion.110
  212.8 49.1 %fusion.73 = f32[32,48,512]{2,1,0:T(8,128)} fusion(f32[32,48,512]{2,1,0:T(8,128)} %bitcast.237, f32[512]{0:T(512)S(1)} %bitcast.356, f32[512]{0:T(512)S(1)} %bitcast.358, f32[512]{0:T(512)S(1)} %bitcast.362, f32[512]{0:T(512)S(1)} %bitcast.364, f32[512]{0:T(512)S(1)} %bitcast.366, f32[512]{0:T(512)S(1)} %bitcast.368, f32[512]{0:T(512)S(1)} %bitcast.370, ...), kind=kLoop, calls=%fused_computation.139 | loop fusion | flops 71565312 | bytes 6401024 | tf_op jit(solution)/shard_map/add | solution.py:53
  261.9 4.7 %multiply_convert_fusion.1 = (bf16[1536,512]{1,0:T(8,128)(2,1)S(1)}, bf16[1536,512]{1,0:T(8,128)(2,1)S(1)}) fusion(f32[32,48,512]{2,1,0:T(8,128)} %fusion.73, pred[1536]{0:T(1024)(128)(4,1)S(1)} %lt.126, f32[1536,1024]{1,0:T(8,128)} %copy-done.3), kind=kLoop, calls=%fused_computation.201 | loop fusion | flops 8650752 | bytes 12584448 | tf_op jit(solution)/shard_map/convert.1
  270.9 4.8 %multiply_reduce_fusion = (f32[512]{0:T(512)S(1)}, f32[1536]{0:T(1024)S(1)}, f32[1536]{0:T(1024)S(1)}, f32[1536,512]{1,0:T(8,128)S(1)}) fusion(bf16[8,4,48,512]{3,2,1,0:T(8,128)(2,1)} %all-to-all-done, f32[1536]{0:T(1024)S(1)} %rsqrt.15, f32[1536]{0:T(1024)S(1)} %div.33, f32[512]{0:T(512)S(1)} %copy-done.41, bf16[512,1024]{1,0:T(8,128)(2,1)} %param.17, ...), kind=kOutput, calls=%fused_computation.166 | convolution fusion | flops 1623978496 | bytes 8941568 | tf_op jit(solution)/shard_map/rf,df->rd/dot_general | solution.py:147
  279.2 5.2 %all-to-all-start.1 = ((bf16[8,4,48,512]{3,2,1,0:T(8,128)(2,1)}), bf16[8,4,48,512]{3,2,1,0:T(8,128)(2,1)}, u32[]{:S(2)}, u32[]{:S(2)}) async-start(bf16[8,4,48,512]{3,2,1,0:T(8,128)(2,1)} %bitcast.73), calls=%async_computation.1 | async-start | bytes 3145728 | tf_op jit(solution)/shard_map/all_to_all | solution.py:152
  286.5 4.5 fusion.102
  292.0 16.2 %compare_and_fusion.1 = (pred[768]{0:T(1024)(128)(4,1)S(1)}, s32[768]{0:T(1024)S(1)}) fusion(s32[768]{0:T(1024)S(1)} %convert_reduce_fusion.1, pred[768]{0:T(1024)(128)(4,1)S(1)} %get-tuple-element.70, pred[768]{0:T(1024)(128)(4,1)S(1)} %get-tuple-element.68, pred[768]{0:T(1024)(128)(4,1)S(1)} %get-tuple-element.69, ...), kind=kLoop, calls=%fused_computation.315 | loop fusion | flops 32256 | bytes 29284 | tf_op jit(solution)/shard_map/jit(_take)/and | solution.py:125
  314.1 21.9 %all-reduce.2 = bf16[512]{0:T(512)(128)(2,1)S(1)} all-reduce(f32[512]{0:T(512)S(1)} %get-tuple-element.9), channel_id=5, replica_groups=mesh['dp'=4,'bucket'=8] {'bucket'}, use_global_device_ids=true, to_apply=%region_56.58.clone | all-reduce | flops 512 | bytes 3072
  339.1 5.9 %all-reduce.5 = (bf16[64,31]{0,1:T(8,128)(2,1)S(1)}, bf16[64]{0:T(256)(128)(2,1)S(1)}) all-reduce(bf16[64,31]{0,1:T(8,128)(2,1)S(1)} %copy.42, bf16[64]{0:T(256)(128)(2,1)S(1)} %dynamic-slice.3), channel_id=1, replica_groups=mesh['dp'=4,'bucket'=8] {'dp'}, use_global_device_ids=true, to_apply=%region_54.56 | all-reduce | flops 2048 | bytes 8192 | tf_op jit(solution)/shard_map/psum | solution.py:171
  346.2 7.7 %reduce-scatter.8.cloned.1.call-done = f32[64,512]{1,0:T(8,128)} async-done(((f32[512,512]{1,0:T(8,128)}), f32[64,512]{1,0:T(8,128)}) %reduce-scatter.8.cloned.1.call-update) | async-done | bytes 131088 | tf_op jit(solution)/shard_map/reduce_scatter | solution.py:164
  357.5 67.6 %reduce-scatter.6.cloned.1.call-done = f32[64,1024]{1,0:T(8,128)} async-done(((f32[512,1024]{1,0:T(8,128)}), f32[64,1024]{1,0:T(8,128)}) %reduce-scatter.6.cloned.1.call-update) | async-done | bytes 262160 | tf_op jit(solution)/shard_map/reduce_scatter | solution.py:163
  428.0 31.1 %all-reduce.9.cloned.1.call-done = (bf16[64,1024]{1,0:T(8,128)(2,1)}, bf16[64,512]{1,0:T(8,128)(2,1)}) async-done(((bf16[64,1024]{1,0:T(8,128)(2,1)}, bf16[64,512]{1,0:T(8,128)(2,1)}), (bf16[64,1024]{1,0:T(8,128)(2,1)}, bf16[64,512]{1,0:T(8,128)(2,1)})) %all-reduce.9.cloned.1.call-update) | async-done | bytes 196624 | tf_op jit(solution)/shard_map/psum | solution.py:169
  (186 shorter events, 54.1 us)
Async XLA Ops:
  7.2 3.6 copy-start
  12.6 10.2 %copy-start.46 = (s32[1,256]{1,0:T(1,128)S(1)}, s32[1,256]{1,0:T(1,128)}, u32[]{:S(2)}) copy-start(s32[1,256]{1,0:T(1,128)} %param.13) | copy-start | bytes 3076
  12.6 12.0 %copy-start.1 = (bf16[768,512]{1,0:T(8,128)(2,1)S(1)}, bf16[768,512]{1,0:T(8,128)(2,1)}, u32[]{:S(2)}) copy-start(bf16[768,512]{1,0:T(8,128)(2,1)} %param.15) | copy-start | bytes 2359300
  15.4 44.4 %all-to-all-start = ((bf16[8,4,48,512]{3,2,1,0:T(8,128)(2,1)}), bf16[8,4,48,512]{3,2,1,0:T(8,128)(2,1)}, u32[]{:S(2)}, u32[]{:S(2)}) async-start(bf16[8,4,48,512]{3,2,1,0:T(8,128)(2,1)} %bitcast.243), calls=%async_computation | async-start | bytes 3145728 | tf_op jit(solution)/shard_map/all_to_all | solution.py:84
  22.7 315.6 %reduce-scatter.10.cloned.1.call-start = ((), (), s32[]{:S(2)}) async-start(), calls=%async_computation.7 | async-start | bytes 294912
  24.5 5.4 %copy-start.9 = (f32[512,31]{0,1:T(8,128)S(1)}, f32[512,31]{0,1:T(8,128)}, u32[]{:S(2)}) copy-start(f32[512,31]{0,1:T(8,128)} %param.18) | copy-start | bytes 190468
  29.9 33.8 %copy-start.41 = (f32[512]{0:T(512)S(1)}, f32[512]{0:T(512)}, u32[]{:S(2)}) copy-start(f32[512]{0:T(512)} %param.16) | copy-start | bytes 6148
  30.0 103.4 %copy-start.45 = (pred[1536]{0:T(1024)(128)(4,1)}, pred[1536]{0:T(1024)(128)(4,1)S(1)}, u32[]{:S(2)}) copy-start(pred[1536]{0:T(1024)(128)(4,1)S(1)} %compare_and_fusion) | copy-start | bytes 4612
  30.1 35.7 %copy-start.47 = (bf16[512,1024]{1,0:T(8,128)(2,1)S(1)}, bf16[512,1024]{1,0:T(8,128)(2,1)}, u32[]{:S(2)}) copy-start(bf16[512,1024]{1,0:T(8,128)(2,1)} %param.17) | copy-start | bytes 3145732
  67.6 2.7 copy-start.3
  67.6 2.7 copy-start.10
  70.3 58.9 %copy-start.40 = (f32[512]{0:T(512)S(1)}, f32[512]{0:T(512)}, u32[]{:S(2)}) copy-start(f32[512]{0:T(512)} %param.19) | copy-start | bytes 6148
  70.3 58.9 %copy-start.42 = (f32[512]{0:T(512)S(1)}, f32[512]{0:T(512)}, u32[]{:S(2)}) copy-start(f32[512]{0:T(512)} %param.20) | copy-start | bytes 6148
  129.2 4.2 copy-start.5
  129.2 4.2 copy-start.48
  133.4 4.3 copy-start.4
  179.0 6.1 %copy-start.44 = (f32[512]{0:T(512)}, f32[512]{0:T(512)S(1)}, u32[]{:S(2)}) copy-start(f32[512]{0:T(512)S(1)} %get-tuple-element.72) | copy-start | bytes 6148
  185.2 15.7 %copy-start.2 = (f32[1536,512]{1,0:T(8,128)}, f32[1536,512]{1,0:T(8,128)S(1)}, u32[]{:S(2)}) copy-start(f32[1536,512]{1,0:T(8,128)S(1)} %get-tuple-element.80) | copy-start | bytes 9437188
  208.4 145.4 %reduce-scatter.8.cloned.1.call-start = ((), (), s32[]{:S(2)}) async-start(), calls=%async_computation.6 | async-start | bytes 1179648 | tf_op jit(solution)/shard_map/reduce_scatter | solution.py:164
  212.5 212.5 %reduce-scatter.6.cloned.1.call-start = ((), (), s32[]{:S(2)}) async-start(), calls=%async_computation.5 | async-start | bytes 2359296 | tf_op jit(solution)/shard_map/reduce_scatter | solution.py:163
  261.9 5.9 %copy-start.7 = (bf16[1536,512]{1,0:T(8,128)(2,1)S(1)}, bf16[1536,512]{1,0:T(8,128)(2,1)}, u32[]{:S(2)}) copy-start(bf16[1536,512]{1,0:T(8,128)(2,1)} %copy-done.6) | copy-start | bytes 4718596
  279.2 5.2 %copy-start.49 = (u32[32]{0:T(128)S(1)}, u32[32]{0:T(128)}, u32[]{:S(2)}) copy-start(u32[32]{0:T(128)} %constant.240) | copy-start | bytes 388
  279.2 76.2 %all-to-all-start.1 = ((bf16[8,4,48,512]{3,2,1,0:T(8,128)(2,1)}), bf16[8,4,48,512]{3,2,1,0:T(8,128)(2,1)}, u32[]{:S(2)}, u32[]{:S(2)}) async-start(bf16[8,4,48,512]{3,2,1,0:T(8,128)(2,1)} %bitcast.73), calls=%async_computation.1 | async-start | bytes 3145728 | tf_op jit(solution)/shard_map/all_to_all | solution.py:152
  284.4 174.7 %all-reduce.9.cloned.1.call-start = ((), (), s32[]{:S(2)}) async-start(), calls=%async_computation.8 | async-start | bytes 393216 | tf_op jit(solution)/shard_map/psum | solution.py:169
  (32 other events, 79.1 us)
Sparse Core Ops, SparseCore 0:
  208.5 61.9 reduce-scatter.9
  273.9 79.8 reduce-scatter.7
  357.4 67.6 reduce-scatter.5
  427.9 31.1 all-reduce.8
where the time goes:
time: 470 us; the launch traced here: 469 us
  other arithmetic  155 us (33%)
  waiting for transfers between devices  136 us (29%)
  blocking collectives  107 us (23%)
  local copies, waits for them, and re-layouts  21.6 us (5%)
  matrix products  20.6 us (4%)
  between operations  15.4 us (3%)
  starting transfers between devices  12.8 us (3%)
    reduce_scatter x1, waiting for transfers between devices, local(): lax.psum_scatter(grad_win, 'bucket', scatter_dimension=0, tiled=True)  67.6 us
    add x1, other arithmetic, conv_backward(): grad_gated + jnp.where(same_back, grad_pad[:, back_start:back_start + len...  49.1 us
    psum x1, blocking collectives, local(): lax.psum((jnp.sum(grad_bn_rows, axis=0), jnp.sum(grad_bn_rows * bn_normed...  41.4 us
    psum x1, blocking collectives, local(): lax.psum((jnp.sum(masked, axis=0), jnp.sum(masked * masked, axis=0)), ('d...  37.9 us
    psum x1, waiting for transfers between devices, local(): lax.psum(row_sums[0].astype(jnp.bfloat16), 'dp').astype(jnp.float32)  31.1 us
    all_to_all x1, waiting for transfers between devices, local(): lax.all_to_all(outgoing, 'bucket', split_axis=0, concat_axis=0, tiled=True)  29.7 us
    reduce_sum x5, other arithmetic, conv_backward(): grad_cols.append(jnp.sum(shifted * grad_conv, axis=(0, 1)))  27.7 us
    unnamed x1, blocking collectives  21.9 us
  transfers between devices with their start and end apart: 6, of which 4 were waited for; matrix products, arithmetic and copies ran while one was open for 24% of the time, Pallas kernels for 0%

commit v1 on v0

--- a/solution.py
+++ b/solution.py
@@ -166,7 +166,7 @@
         lax.psum_scatter(grad_ln, "bucket", scatter_dimension=0, tiled=True),
     )
     shares = (
-        lax.psum(row_sums[0].astype(jnp.bfloat16), "dp").astype(jnp.float32),
+        jnp.sum(lax.all_gather(row_sums[0].astype(jnp.bfloat16), "dp"), axis=0).astype(jnp.float32),
         lax.psum(row_sums[1].astype(jnp.bfloat16), "dp").astype(jnp.float32),
         lax.psum(row_sums[2].astype(jnp.bfloat16), "dp").astype(jnp.float32),
         lax.psum(row_sums[3].astype(jnp.bfloat16), "dp").astype(jnp.float32),

time: 470 us -> 401 us (0.85)
  waiting for transfers between devices: 136 us -> 57.9 us
  blocking collectives: 107 us -> 115 us
    reduce_scatter x1, waiting for transfers between devices: 67.6 us -> 28.1 us  [local(): lax.psum_scatter(grad_win, 'bucket', scatter_dimension=0, tiled=True)]
    psum x1, waiting for transfers between devices: 31.1 us -> 0.01 us  [local(): lax.psum(row_sums[1].astype(jnp.bfloat16), 'dp').astype(jnp.float32)]
    reduce_scatter x1, waiting for transfers between devices: 7.68 us -> 0.01 us  [local(): lax.psum_scatter(grad_wout, 'bucket', scatter_dimension=0, tiled=True)]
    all_gather x0 -> x1, blocking collectives: none -> 7.14 us  [local(): lax.all_gather(row_sums[0].astype(jnp.bfloat16), 'dp')]
  transfers between devices with their start and end apart: 6 -> 6, of which waited for: 4 -> 2; matrix products, arithmetic and copies ran while one was open for 24% -> 37% of each run, Pallas kernels for 0% -> 0%
where the time goes in v1:
time: 401 us; the launch traced here: 400 us
  other arithmetic  153 us (38%)
  blocking collectives  115 us (29%)
  waiting for transfers between devices  57.9 us (14%)
  matrix products  23.5 us (6%)
  local copies, waits for them, and re-layouts  22.7 us (6%)
  between operations  15.3 us (4%)
  starting transfers between devices  12.6 us (3%)
    add x1, other arithmetic, conv_backward(): grad_gated + jnp.where(same_back, grad_pad[:, back_start:back_start + len...  47 us
    psum x1, blocking collectives, local(): lax.psum((jnp.sum(grad_bn_rows, axis=0), jnp.sum(grad_bn_rows * bn_normed...  41.7 us
    psum x1, blocking collectives, local(): lax.psum((jnp.sum(masked, axis=0), jnp.sum(masked * masked, axis=0)), ('d...  37.9 us
    all_to_all x1, waiting for transfers between devices, local(): lax.all_to_all(outgoing, 'bucket', split_axis=0, concat_axis=0, tiled=True)  29.7 us
    reduce_scatter x1, waiting for transfers between devices, local(): lax.psum_scatter(grad_win, 'bucket', scatter_dimension=0, tiled=True)  28.1 us
    reduce_sum x5, other arithmetic, conv_backward(): grad_cols.append(jnp.sum(shifted * grad_conv, axis=(0, 1)))  27.7 us
    unnamed x1, blocking collectives  21.8 us
    reduce_sum x1, other arithmetic, local(): jnp.sum(masked, axis=0)  20.7 us
  transfers between devices with their start and end apart: 6, of which 2 were waited for; matrix products, arithmetic and copies ran while one was open for 37% of the time, Pallas kernels for 0%

profile of v1, /device:TPU:0, one launch (start us, length us, event | category | flops | bytes accessed | tf_op | source)
XLA Modules:
  0.0 399.7 jit_solution(7504325124869062944)
XLA Ops:
  15.4 7.3 %all-to-all-start = ((bf16[8,4,48,512]{3,2,1,0:T(8,128)(2,1)}), bf16[8,4,48,512]{3,2,1,0:T(8,128)(2,1)}, u32[]{:S(2)}, u32[]{:S(2)}) async-start(bf16[8,4,48,512]{3,2,1,0:T(8,128)(2,1)} %bitcast.244), calls=%async_computation | async-start | bytes 3145728 | tf_op jit(solution)/shard_map/all_to_all | solution.py:84
  24.5 5.4 %gather_fusion.1 = bf16[1536,512]{1,0:T(8,128)(2,1)} fusion(bf16[768,512]{1,0:T(8,128)(2,1)S(1)} %copy-done.1, s32[2048]{0:T(1024)S(1)} %pad_clamp_fusion), kind=kCustom, calls=%fused_computation.3 | custom fusion | bytes 3151872 | tf_op jit(solution)/shard_map/jit(_take)/gather | solution.py:103
  30.0 29.7 %all-to-all-done = bf16[8,4,48,512]{3,2,1,0:T(8,128)(2,1)} async-done(((bf16[8,4,48,512]{3,2,1,0:T(8,128)(2,1)}), bf16[8,4,48,512]{3,2,1,0:T(8,128)(2,1)}, u32[]{:S(2)}, u32[]{:S(2)}) %all-to-all-start) | async-done | bytes 1572896 | tf_op jit(solution)/shard_map/all_to_all | solution.py:84
  72.9 20.7 %select_reduce_fusion = (f32[512]{0:T(512)S(1)}, f32[512]{0:T(512)S(1)}, f32[32,48,512]{2,1,0:T(8,128)}) fusion(pred[32,48]{1,0:T(8,128)(4,1)S(1)} %iota_compare_fusion.3, f32[512]{0:T(512)S(1)} %bitcast.357, pred[32,48]{1,0:T(8,128)(4,1)S(1)} %bitcast.325, f32[512]{0:T(512)S(1)} %bitcast.359, pred[32,48]{1,0:T(8,128)(4,1)S(1)} %bitcast.322, ...), kind=kLoop, calls=%fused_computation.243 | loop fusion | flops 99089408 | bytes 4833792 | tf_op jit(solution)/shard_map/reduce_sum | solution.py:115
  93.6 37.9 %all-reduce.4 = (f32[512]{0:T(512)S(1)}, f32[512]{0:T(512)S(1)}) all-reduce(f32[512]{0:T(512)S(1)} %get-tuple-element.42, f32[512]{0:T(512)S(1)} %get-tuple-element.41), channel_id=1, replica_groups=mesh['dp'=4,'bucket'=8] {'dp','bucket'}, use_global_device_ids=true, to_apply=%region_11.13 | all-reduce | flops 1024 | bytes 8192 | tf_op jit(solution)/shard_map/psum | solution.py:114
  131.5 4.7 %multiply_convert_fusion.2 = (bf16[1536,512]{1,0:T(8,128)(2,1)S(1)}, f32[1536,512]{1,0:T(8,128)}) fusion(f32[512]{0:T(512)S(1)} %copy-done.41, f32[512]{0:T(512)S(1)} %copy-done.39, f32[512]{0:T(512)S(1)} %get-tuple-element.82, f32[512]{0:T(512)S(1)} %get-tuple-element.125, f32[32,48,512]{2,1,0:T(8,128)} %get-tuple-element.89), kind=kLoop, calls=%fused_computation.204 | loop fusion | flops 7077888 | bytes 7872512 | tf_op jit(solution)/shard_map/convert_element_type | solution.py:123
  139.5 5.5 %fusion.111 = (f32[512]{0:T(512)S(1)}, f32[512]{0:T(512)S(1)}, f32[1536,512]{1,0:T(8,128)}) fusion(f32[1536,512]{1,0:T(8,128)} %get-tuple-element.88, f32[512]{0:T(512)S(1)} %copy-done.41, f32[512]{0:T(512)S(1)} %copy-done.39, bf16[512,512]{1,0:T(8,128)(2,1)} %param.21, bf16[1536,512]{1,0:T(8,128)(2,1)} %gather_fusion.1, ...), kind=kOutput, calls=%fused_computation.339 | convolution fusion | flops 817101824 | bytes 8399872 | tf_op jit(solution)/shard_map/re,de->rd/dot_general | solution.py:127
  145.0 41.7 %all-reduce.3 = (f32[512]{0:T(512)S(1)}, f32[512]{0:T(512)S(1)}) all-reduce(f32[512]{0:T(512)S(1)} %get-tuple-element.45, f32[512]{0:T(512)S(1)} %get-tuple-element.44), channel_id=1, replica_groups=mesh['dp'=4,'bucket'=8] {'dp','bucket'}, use_global_device_ids=true, to_apply=%region_15.17 | all-reduce | flops 1024 | bytes 8192 | tf_op jit(solution)/shard_map/psum | solution.py:129
  187.3 5.5 %multiply_reduce_fusion.16 = (f32[512]{0:T(512)S(1)}, f32[1536,512]{1,0:T(8,128)S(1)}) fusion(f32[1536,512]{1,0:T(8,128)} %get-tuple-element.88, f32[512]{0:T(512)S(1)} %get-tuple-element.162, f32[1536,512]{1,0:T(8,128)} %get-tuple-element.160, f32[512]{0:T(512)S(1)} %get-tuple-element.163, f32[512]{0:T(512)S(1)} %get-tuple-element.81, ...), kind=kLoop, calls=%fused_computation.182 | loop fusion | flops 11009536 | bytes 15738368 | tf_op jit(solution)/shard_map/reduce_sum | solution.py:49
  192.9 7.1 %multiply_reduce_fusion.10 = (f32[512]{0:T(512)S(1)}, f32[512]{0:T(512)S(1)}, f32[512]{0:T(512)S(1)}, f32[512]{0:T(512)S(1)}, f32[512]{0:T(512)S(1)}, /*index=5*...) fusion(f32[32,48,512]{2,1,0:T(8,128)S(1)} %bitcast.234, pred[32,48]{1,0:T(8,128)(4,1)S(1)} %bitcast.299, ...), kind=kLoop, calls=%fused_computation.176 | loop fusion | flops 28306944 | bytes 4750848 | tf_op jit(solution)/shard_map/reduce_sum | solution.py:49
  200.0 6.7 %multiply_reduce_fusion.20 = (f32[512]{0:T(512)S(1)}, f32[512]{0:T(512)S(1)}, f32[512]{0:T(512)S(1)}, f32[512]{0:T(512)S(1)}, f32[512]{0:T(512)S(1)}, /*index=5*...) fusion(f32[32,48,512]{2,1,0:T(8,128)S(1)} %bitcast.235, pred[32,48]{1,0:T(8,128)(4,1)S(1)} %bitcast.272, ...), kind=kLoop, calls=%fused_computation.186 | loop fusion | flops 28306944 | bytes 4750848 | tf_op jit(solution)/shard_map/reduce_sum | solution.py:49
  208.6 6.5 %multiply_reduce_fusion.1 = (f32[512]{0:T(512)S(1)}, f32[512]{0:T(512)S(1)}, f32[512]{0:T(512)S(1)}, f32[512]{0:T(512)S(1)}, f32[512]{0:T(512)S(1)}, /*index=5*/...) fusion(f32[32,48,512]{2,1,0:T(8,128)S(1)} %bitcast.237, pred[32,48]{1,0:T(8,128)(4,1)S(1)} %bitcast.326, ...), kind=kLoop, calls=%fused_computation.167 | loop fusion | flops 28306944 | bytes 4750848 | tf_op jit(solution)/shard_map/reduce_sum | solution.py:49
  216.2 47.0 %fusion.73 = f32[32,48,512]{2,1,0:T(8,128)} fusion(f32[32,48,512]{2,1,0:T(8,128)} %bitcast.238, f32[512]{0:T(512)S(1)} %bitcast.358, f32[512]{0:T(512)S(1)} %bitcast.360, f32[512]{0:T(512)S(1)} %bitcast.364, f32[512]{0:T(512)S(1)} %bitcast.366, f32[512]{0:T(512)S(1)} %bitcast.368, f32[512]{0:T(512)S(1)} %bitcast.370, f32[512]{0:T(512)S(1)} %bitcast.372, ...), kind=kLoop, calls=%fused_computation.139 | loop fusion | flops 71565312 | bytes 6401024 | tf_op jit(solution)/shard_map/add | solution.py:53
  263.3 5.8 %multiply_convert_fusion.1 = (bf16[1536,512]{1,0:T(8,128)(2,1)}, bf16[1536,512]{1,0:T(8,128)(2,1)}) fusion(f32[32,48,512]{2,1,0:T(8,128)} %fusion.73, pred[1536]{0:T(1024)(128)(4,1)S(1)} %lt.126, f32[1536,1024]{1,0:T(8,128)} %copy-done.3), kind=kLoop, calls=%fused_computation.201 | loop fusion | flops 8650752 | bytes 12584448 | tf_op jit(solution)/shard_map/convert.2
  270.9 5.1 %fusion.95 = f32[512,1024]{1,0:T(8,128)} fusion(bf16[1536,512]{1,0:T(8,128)(2,1)S(1)} %copy-done.7, bf16[1536,512]{1,0:T(8,128)(2,1)} %get-tuple-element.91, bf16[1536,512]{1,0:T(8,128)(2,1)} %get-tuple-element.90), kind=kOutput, calls=%fused_computation.246 | convolution fusion | flops 1616904192 | bytes 6815744 | tf_op jit(solution)/shard_map/rd,rf->df/dot_general | solution.py:146
  276.0 5.3 %multiply_reduce_fusion = (f32[512]{0:T(512)S(1)}, f32[1536]{0:T(1024)S(1)}, f32[1536]{0:T(1024)S(1)}, f32[1536,512]{1,0:T(8,128)S(1)}) fusion(bf16[8,4,48,512]{3,2,1,0:T(8,128)(2,1)} %all-to-all-done, f32[1536]{0:T(1024)S(1)} %rsqrt.15, f32[1536]{0:T(1024)S(1)} %div.33, f32[512]{0:T(512)S(1)} %copy-done.40, bf16[512,1024]{1,0:T(8,128)(2,1)} %param.17, ...), kind=kOutput, calls=%fused_computation.166 | convolution fusion | flops 1623978496 | bytes 8941568 | tf_op jit(solution)/shard_map/rf,df->rd/dot_general | solution.py:147
  281.4 3.4 select_convert_fusion
  284.8 5.0 %all-to-all-start.1 = ((bf16[8,4,48,512]{3,2,1,0:T(8,128)(2,1)}), bf16[8,4,48,512]{3,2,1,0:T(8,128)(2,1)}, u32[]{:S(2)}, u32[]{:S(2)}) async-start(bf16[8,4,48,512]{3,2,1,0:T(8,128)(2,1)} %bitcast.73), calls=%async_computation.1 | async-start | bytes 3145728 | tf_op jit(solution)/shard_map/all_to_all | solution.py:152
  291.8 4.5 %fusion.102 = (s32[768]{0:T(1024)S(1)}, s32[768,1]{0,1:T(1,128)S(1)}) fusion(s32[]{:T(128)} %bitcast.25, s32[]{:T(128)} %bitcast.26, s32[]{:T(128)} %bitcast.27, s32[]{:T(128)} %bitcast.28, s32[]{:T(128)} %bitcast.29, s32[]{:T(128)} %bitcast.31, s32[]{:T(128)} %bitcast.30, s32[768]{0:T(1024)S(1)} %get-tuple-element.124, s32[768]{0:T(1024)S(1)} %get-tuple-element.123), kind=kLoop, calls=%fused_computation.316 | loop fusion | flops 10752 | bytes 12316 | tf_op jit(solution)/shard_map/jit(_take)/gather | solution.py:94
  297.2 15.7 %compare_and_fusion.1 = (pred[768]{0:T(1024)(128)(4,1)S(1)}, s32[768]{0:T(1024)S(1)}) fusion(s32[768]{0:T(1024)S(1)} %convert_reduce_fusion.1, pred[768]{0:T(1024)(128)(4,1)S(1)} %get-tuple-element.70, pred[768]{0:T(1024)(128)(4,1)S(1)} %get-tuple-element.68, pred[768]{0:T(1024)(128)(4,1)S(1)} %get-tuple-element.69, ...), kind=kLoop, calls=%fused_computation.315 | loop fusion | flops 32256 | bytes 29284 | tf_op jit(solution)/shard_map/jit(_take)/and | solution.py:125
  318.8 21.8 %all-reduce.2 = bf16[512]{0:T(512)(128)(2,1)S(1)} all-reduce(f32[512]{0:T(512)S(1)} %get-tuple-element.9), channel_id=6, replica_groups=mesh['dp'=4,'bucket'=8] {'bucket'}, use_global_device_ids=true, to_apply=%region_56.58.clone | all-reduce | flops 512 | bytes 3072
  343.7 6.3 %all-reduce.5 = (bf16[64,31]{0,1:T(8,128)(2,1)S(1)}, bf16[64]{0:T(256)(128)(2,1)S(1)}) all-reduce(bf16[64,31]{0,1:T(8,128)(2,1)S(1)} %copy.42, bf16[64]{0:T(256)(128)(2,1)S(1)} %dynamic-slice.3), channel_id=1, replica_groups=mesh['dp'=4,'bucket'=8] {'dp'}, use_global_device_ids=true, to_apply=%region_54.56 | all-reduce | flops 2048 | bytes 8192 | tf_op jit(solution)/shard_map/psum | solution.py:171
  356.1 28.1 %reduce-scatter.6.cloned.1.call-done = f32[64,1024]{1,0:T(8,128)} async-done(((f32[512,1024]{1,0:T(8,128)}), f32[64,1024]{1,0:T(8,128)}) %reduce-scatter.6.cloned.1.call-update) | async-done | bytes 262160 | tf_op jit(solution)/shard_map/reduce_scatter | solution.py:163
  385.2 7.1 %all-gather = bf16[256,1024]{1,0:T(8,128)(2,1)S(1)} all-gather(bf16[64,1024]{1,0:T(8,128)(2,1)S(1)} %convert_element_type.233), channel_id=2, replica_groups=mesh['dp'=4,'bucket'=8] {'dp'}, dimensions={0}, use_global_device_ids=true | all-gather | bytes 655360 | tf_op jit(solution)/shard_map/all_gather | solution.py:169
  (180 shorter events, 50.4 us)
Async XLA Ops:
  7.2 3.6 copy-start
  12.6 10.2 %copy-start.44 = (s32[1,256]{1,0:T(1,128)S(1)}, s32[1,256]{1,0:T(1,128)}, u32[]{:S(2)}) copy-start(s32[1,256]{1,0:T(1,128)} %param.13) | copy-start | bytes 3076
  12.6 12.0 %copy-start.1 = (bf16[768,512]{1,0:T(8,128)(2,1)S(1)}, bf16[768,512]{1,0:T(8,128)(2,1)}, u32[]{:S(2)}) copy-start(bf16[768,512]{1,0:T(8,128)(2,1)} %param.15) | copy-start | bytes 2359300
  15.4 44.4 %all-to-all-start = ((bf16[8,4,48,512]{3,2,1,0:T(8,128)(2,1)}), bf16[8,4,48,512]{3,2,1,0:T(8,128)(2,1)}, u32[]{:S(2)}, u32[]{:S(2)}) async-start(bf16[8,4,48,512]{3,2,1,0:T(8,128)(2,1)} %bitcast.244), calls=%async_computation | async-start | bytes 3145728 | tf_op jit(solution)/shard_map/all_to_all | solution.py:84
  22.7 246.4 %reduce-scatter.8.cloned.1.call-start = ((), (), s32[]{:S(2)}) async-start(), calls=%async_computation.6 | async-start | bytes 1179648 | tf_op jit(solution)/shard_map/reduce_scatter | solution.py:164
  24.5 5.4 %copy-start.8 = (f32[512,31]{0,1:T(8,128)S(1)}, f32[512,31]{0,1:T(8,128)}, u32[]{:S(2)}) copy-start(f32[512,31]{0,1:T(8,128)} %param.18) | copy-start | bytes 190468
  29.9 33.8 %copy-start.40 = (f32[512]{0:T(512)S(1)}, f32[512]{0:T(512)}, u32[]{:S(2)}) copy-start(f32[512]{0:T(512)} %param.16) | copy-start | bytes 6148
  69.9 2.7 copy-start.3
  70.0 2.7 copy-start.9
  70.0 2.6 copy-start.10
  70.0 2.6 copy-start.11
  70.0 2.6 copy-start.12
  70.0 2.6 copy-start.13
  72.6 58.8 %copy-start.39 = (f32[512]{0:T(512)S(1)}, f32[512]{0:T(512)}, u32[]{:S(2)}) copy-start(f32[512]{0:T(512)} %param.19) | copy-start | bytes 6148
  72.6 58.9 %copy-start.41 = (f32[512]{0:T(512)S(1)}, f32[512]{0:T(512)}, u32[]{:S(2)}) copy-start(f32[512]{0:T(512)} %param.20) | copy-start | bytes 6148
  131.5 5.8 %copy-start.4 = (bf16[1536,512]{1,0:T(8,128)(2,1)S(1)}, bf16[1536,512]{1,0:T(8,128)(2,1)}, u32[]{:S(2)}) copy-start(bf16[1536,512]{1,0:T(8,128)(2,1)} %gather_fusion.1) | copy-start | bytes 4718596
  139.5 203.4 %reduce-scatter.10.cloned.1.call-start = ((), (), s32[]{:S(2)}) async-start(), calls=%async_computation.8 | async-start | bytes 294912
  186.8 6.1 %copy-start.43 = (f32[512]{0:T(512)}, f32[512]{0:T(512)S(1)}, u32[]{:S(2)}) copy-start(f32[512]{0:T(512)S(1)} %get-tuple-element.72) | copy-start | bytes 6148
  192.9 15.7 %copy-start.2 = (f32[1536,512]{1,0:T(8,128)}, f32[1536,512]{1,0:T(8,128)S(1)}, u32[]{:S(2)}) copy-start(f32[1536,512]{1,0:T(8,128)S(1)} %get-tuple-element.78) | copy-start | bytes 9437188
  216.2 135.0 %all-reduce.8.cloned.1.call-start = ((), (), s32[]{:S(2)}) async-start(), calls=%async_computation.7 | async-start | bytes 131072 | tf_op jit(solution)/shard_map/psum | solution.py:170
  263.2 7.7 %copy-start.7 = (bf16[1536,512]{1,0:T(8,128)(2,1)S(1)}, bf16[1536,512]{1,0:T(8,128)(2,1)}, u32[]{:S(2)}) copy-start(bf16[1536,512]{1,0:T(8,128)(2,1)} %copy-done.6) | copy-start | bytes 4718596
  270.7 113.6 %reduce-scatter.6.cloned.1.call-start = ((), (), s32[]{:S(2)}) async-start(), calls=%async_computation.5 | async-start | bytes 2359296 | tf_op jit(solution)/shard_map/reduce_scatter | solution.py:163
  284.8 5.0 %copy-start.45 = (u32[32]{0:T(128)S(1)}, u32[32]{0:T(128)}, u32[]{:S(2)}) copy-start(u32[32]{0:T(128)} %constant.241) | copy-start | bytes 388
  284.8 67.9 %all-to-all-start.1 = ((bf16[8,4,48,512]{3,2,1,0:T(8,128)(2,1)}), bf16[8,4,48,512]{3,2,1,0:T(8,128)(2,1)}, u32[]{:S(2)}, u32[]{:S(2)}) async-start(bf16[8,4,48,512]{3,2,1,0:T(8,128)(2,1)} %bitcast.73), calls=%async_computation.1 | async-start | bytes 3145728 | tf_op jit(solution)/shard_map/all_to_all | solution.py:152
  (28 other events, 67.9 us)
Sparse Core Ops, SparseCore 0:
  139.6 65.3 reduce-scatter.7
  216.3 61.8 reduce-scatter.9
  281.0 30.5 all-reduce.7
  315.1 69.1 reduce-scatter.5
